TPU v7x, 256 devices: a whole 4x4x8 slice. The times are simulated.
256 devices in a mesh: ctx: 128 (over z, y_hi, x, core), head: 2 (over y_lo).
Axes of the slice: x: 4, y: 4 (y_hi: 2, y_lo: 2; y = y_hi * 2 + y_lo), z: 8, core: 2. Of those that a mesh axis runs over, the one named last changes fastest.
Arguments:
- queries: bfloat16 [2, 16384, 2048], P(None, 'ctx', 'head'), may hold values from -8 to 8
- keys_values: bfloat16 [2, 2, 16384, 512], P(None, None, 'ctx', 'head'), may hold values from -12 to 12
- grad_layer: bfloat16 [2, 16384, 4096], P(None, 'ctx'), may hold values from -0.29882812 to 0.29882812
- out_proj: bfloat16 [4096, 2048], P('ctx', 'head'), may hold values from -0.125 to 0.125
- doc_layout: int32 [3, 16384], P(None, 'ctx'), may hold values from 0 to 16384, as said below
Outputs:
- layer_out: bfloat16 [2, 16384, 4096], P(None, 'ctx', 'head')
- grad_queries: float32 [2, 16384, 2048], P(None, 'ctx', 'head')
- grad_keys_values: float32 [2, 2, 16384, 512], P(None, None, 'ctx', 'head')
Inputs may be any that keep to these rules, and one draw needn't show every extreme that they name: doc_layout[0, p] and doc_layout[1, p] are the first position and one past the last position of the document that holds position p; documents are consecutive runs covering all 16384 positions, each starting at a multiple of 32 and holding a multiple of 32 positions, at most 896, one of exactly 896; doc_layout[2, p] is that document's diffusion block size, a power of two from 4 to 32, and the document of 896 positions has 32.
All inputs are finite; a program needn't handle non-finite values.
Results may differ from a plain program's by a relative error of at most 0.009.
Values may be sent and summed in bfloat16 or wider, within the bound.
A program may use at most 64 MiB of HBM per device.

v0:
```python
import functools
import math

import jax
import jax.numpy as jnp
from jax import lax
from jax.experimental import pallas as pl
from jax.experimental.pallas import tpu as pltpu
from jax.sharding import PartitionSpec as P

F32 = jnp.float32
BF16 = jnp.bfloat16
MESH = pl.DeviceIdType.MESH
NEG = -1e30
SCALE = 128 ** -0.5
EXP2 = SCALE * math.log2(math.e)

NZ, NY, NX = 8, 2, 4
SUBS = (0, 3, 1, 2)
PLANES = (0, 7, 1, 6, 2, 5, 3, 4)


def nt(a, b):
    return lax.dot_general(a, b, (((1,), (1,)), ((), ())), preferred_element_type=F32)


def nn(a, b):
    return lax.dot_general(a, b, (((1,), (0,)), ((), ())), preferred_element_type=F32)


def kernel(
    q_hbm, kv_hbm, g_hbm, w_hbm, lay_hbm,
    out_hbm, dq_hbm, dkv_hbm,
    wbuf, qs, kvw, kvn, gbuf, lay, bias, bnoisy, st, pt, dst, vt, kt,
    att, gacc, lrow, lcol, gs, dl, ypart, ysend, yrecv, yout,
    stage, evens, col, comb, ret, own, dqv, dkvv,
    dsem, ks, kr, ws, wr, pps, ppr, es, er, rs, rr,
):
    ctx = lax.axis_index("ctx")
    hd = lax.axis_index("head")
    core = lax.rem(ctx, 2)
    x = lax.rem(lax.div(ctx, 2), NX)
    yh = lax.rem(lax.div(ctx, 8), NY)
    z = lax.div(ctx, 16)

    def place(z_, y_, x_):
        return ((z_ * NY + y_) * NX + x_) * 2 + core

    xs = [lax.rem(x + d, NX) for d in range(NX)]
    zs = [lax.rem(z + d, NZ) for d in range(NZ)]
    dev_y = (place(z, 1 - yh, x), hd)
    dev_x = [(place(z, yh, xs[1]), hd), (place(z, yh, xs[3]), hd)]
    dev_z = [(place(zs[1], yh, x), hd), (place(zs[7], yh, x), hd)]
    dev_pair = (ctx + 1 - 2 * core, hd)
    dev_head = (ctx, 1 - hd)
    later = [(lax.rem(ctx + 2 * k, 128), hd) for k in range(4)]
    earlier = [(lax.rem(ctx + 128 - 2 * k, 128), hd) for k in range(4)]
    dev_seven = (lax.rem(ctx + 121 + 14 * core, 128), hd)

    def remote(src, dst_ref, send, recv, device):
        return pltpu.make_async_remote_copy(
            src_ref=src, dst_ref=dst_ref, send_sem=send, recv_sem=recv,
            device_id=device, device_id_type=MESH,
        )

    def fetch(src, dst_ref, sem):
        copy = pltpu.make_async_copy(src, dst_ref, sem)
        copy.start()
        return copy

    get_w = fetch(w_hbm, wbuf.at[z, yh, x, core], dsem.at[0])
    get_kv = fetch(kv_hbm.at[:, 1], kvw.at[0], dsem.at[1])
    get_kn = fetch(kv_hbm.at[:, 0], kvn, dsem.at[2])
    get_lay = fetch(lay_hbm, lay, dsem.at[3])
    for copy_id in range(2):
        for head in range(8):
            pb = (head // 4) * 4 + copy_id * 2 + (head % 4) // 2
            fetch(
                q_hbm.at[copy_id, :, pl.ds(head * 128, 128)],
                qs.at[pb, pl.ds((head % 2) * 128, 128)],
                dsem.at[4],
            )
    get_g = fetch(g_hbm, gbuf, dsem.at[5])

    barrier = pltpu.get_barrier_semaphore()
    meet = [dev_y, *dev_x, *dev_z, dev_pair, dev_head, *later[1:], *earlier[1:], dev_seven]
    for device in meet:
        pl.semaphore_signal(barrier, inc=1, device_id=device, device_id_type=MESH)
    pl.semaphore_wait(barrier, len(meet))

    own_kv = kv_hbm.at[:, 1]
    kv_far = [remote(own_kv, kvw.at[2 * k], ks.at[k], kr.at[2 * k], later[k]) for k in (1, 2, 3)]
    kv_seven = remote(own_kv, kvw.at[7], ks.at[0], kr.at[7], dev_seven)
    kv_own = remote(own_kv, kvw.at[1], ks.at[0], kr.at[1], dev_pair)

    w_first = remote(w_hbm, wbuf.at[z, yh, x, core], ws.at[0], wr.at[0], dev_y)
    w_first.start()

    @pl.when(core == 0)
    def _():
        kv_own.start()

    for copy in kv_far:
        copy.start()

    @pl.when(core == 1)
    def _():
        kv_seven.start()

    def kv_pass(k):
        kv_far[k - 1].wait_recv()

        @pl.when(core == 0)
        def _():
            remote(
                kvw.at[2 * k], kvw.at[2 * k + 1], ks.at[3 + k], kr.at[2 * k + 1], dev_pair
            ).start()

        @pl.when(core == 1)
        def _():
            remote(
                kvw.at[2 * k], kvw.at[2 * k - 1], ks.at[3 + k], kr.at[2 * k - 1], dev_pair
            ).start()

    def kv_odd(slot):
        remote(kvw.at[slot], kvw.at[slot], ks.at[0], kr.at[slot], dev_pair).wait_recv()

    sent = ([], [])

    def send_w(core_id, view, device, recv):
        n = len(sent[core_id]) + 1
        src = view()
        remote(src, src, ws.at[n], wr.at[recv], device).start()
        sent[core_id].append(view)

    def wait_w(src, recv):
        remote(src, src, ws.at[0], wr.at[recv], dev_y).wait_recv()

    def passed(core_id, n):
        src = wbuf.at[zs[PLANES[n]], :, :, core_id]
        return remote(src, src, pps.at[n], ppr.at[n], dev_pair)

    def pass_plane(core_id, n):
        passed(core_id, n).start()

    def sub0(dz, dx):
        return wbuf.at[zs[dz], :, xs[dx], 0]

    def zrecv0(way, hop, s):
        return 5 + (way * 4 + hop - 1) * 4 + s

    def ticks0():
        def first():
            get_w.wait()
            w_first.wait_recv()
            for way in range(2):
                send_w(0, lambda: sub0(0, 0), dev_x[way], 1 + way)
            for way in range(2):
                send_w(0, lambda: sub0(0, 0), dev_z[way], zrecv0(way, 1, 0))

        def second():
            for way, (dx, half) in enumerate(((3, 0), (1, 1))):
                wait_w(sub0(0, dx), 1 + way)
                send_w(0, lambda dx=dx, half=half: wbuf.at[z, half, xs[dx], 0], dev_x[way], 3 + way)
                for zway in range(2):
                    send_w(0, lambda dx=dx: sub0(0, dx), dev_z[zway], zrecv0(zway, 1, 1 + way))

        def third():
            for way in range(2):
                wait_w(wbuf.at[z, way, xs[2], 0], 3 + way)
            for way in range(2):
                send_w(0, lambda: sub0(0, 2), dev_z[way], zrecv0(way, 1, 3))
            pass_plane(0, 0)

        def hop_step(hop, s):
            for way in range(2):
                dz = (8 - hop) if way == 0 else hop
                half = (0, 1) if way == 0 else (2, 3)
                if hop == 4 and s not in half:
                    continue
                wait_w(sub0(dz, SUBS[s]), zrecv0(way, hop, s))
                if hop < 3 or (hop == 3 and s in half):
                    send_w(0, lambda dz=dz: sub0(dz, SUBS[s]), dev_z[way], zrecv0(way, hop + 1, s))
            if s == 3 and hop < 4:
                pass_plane(0, 2 * hop - 1)
                pass_plane(0, 2 * hop)
            if s == 3 and hop == 4:
                pass_plane(0, 7)

        yield first
        yield second
        yield third
        for hop in range(1, 4):
            for s in range(4):
                yield functools.partial(hop_step, hop, s)

        def last():
            for s in range(4):
                hop_step(4, s)

        yield last

    def ticks1():
        def zblock(dz):
            return wbuf.at[zs[dz], :, x, 1]

        def xrecv(n, kind, way):
            return 9 + n * 4 + kind * 2 + way

        def x1(n):
            for way in range(2):
                send_w(1, lambda: zblock(PLANES[n]), dev_x[way], xrecv(n, 0, way))

        def x2(n):
            dz = PLANES[n]
            for way, (dx, half) in enumerate(((3, 0), (1, 1))):
                wait_w(wbuf.at[zs[dz], :, xs[dx], 1], xrecv(n, 0, way))
                send_w(1, lambda dx=dx, half=half: wbuf.at[zs[dz], half, xs[dx], 1], dev_x[way], xrecv(n, 1, way))

        def done(n):
            for way in range(2):
                wait_w(wbuf.at[zs[PLANES[n]], way, xs[2], 1], xrecv(n, 1, way))
            pass_plane(1, n)

        def zhop(hop):
            for way in range(2):
                dz = (8 - hop) if way == 0 else hop
                if hop == 4:
                    wait_w(wbuf.at[zs[4], way, x, 1], 1 + way * 4 + 3)
                    continue
                wait_w(zblock(dz), 1 + way * 4 + hop - 1)

                def view(dz=dz, way=way):
                    return zblock(dz) if hop < 3 else wbuf.at[zs[dz], way, x, 1]

                send_w(1, view, dev_z[way], 1 + way * 4 + hop)

        def first():
            get_w.wait()
            w_first.wait_recv()
            for way in range(2):
                send_w(1, lambda: zblock(0), dev_z[way], 1 + way * 4)
            x1(0)

        plan = [
            [(zhop, 1), (x1, 1), (x1, 2)],
            [(x2, 0)],
            [(zhop, 2), (x1, 3), (x1, 4)],
            [(x2, 1), (x2, 2), (done, 0)],
            [(zhop, 3), (x1, 5), (x1, 6)],
            [(x2, 3)],
            [(done, 1), (done, 2), (zhop, 4), (x1, 7)],
            [(x2, 4)],
            [(x2, 5)],
            [(done, 3), (done, 4), (x2, 6)],
            [(x2, 7)],
            [(done, 5)],
            [(done, 6)],
            [(done, 7)],
            [],
        ]

        def run(steps):
            for step, value in steps:
                step(value)

        yield first
        for steps in plan:
            yield functools.partial(run, steps)

    zero_ticks, one_ticks = list(ticks0()), list(ticks1())
    assert len(zero_ticks) == len(one_ticks) == 16

    def tick(n):
        pl.when(core == 0)(zero_ticks[n])
        pl.when(core == 1)(one_ticks[n])

    get_lay.wait()
    first = ctx * 128
    starts, ends, sizes = lay[0:1, :], lay[1:2, :], lay[2:3, :]
    query = first + lax.broadcasted_iota(jnp.int32, (1, 128), 1)
    base = query & (-sizes)
    row = first + lax.broadcasted_iota(jnp.int32, (128, 128), 0)
    inside = (row >= starts) & (row < ends)
    bias[0, 0:128, :] = jnp.where(inside & (row < base), 0.0, NEG)
    bias[1, 0:128, :] = jnp.where(inside & (row < base + sizes), 0.0, NEG)
    bnoisy[...] = jnp.where(inside & (row >= base) & (row < base + sizes), 0.0, NEG)
    for slot in range(1, 8):
        far = jnp.where(row - slot * 128 >= starts, 0.0, NEG)
        bias[0, slot * 128:(slot + 1) * 128, :] = far
        bias[1, slot * 128:(slot + 1) * 128, :] = far

    tick(0)
    pltpu.make_async_copy(qs, qs, dsem.at[4]).wait()
    get_kv.wait()
    get_kn.wait()

    def lanes(group):
        return pl.ds(pl.multiple_of(group * 128, 128), 128)

    def keys_of(pair, kind, group):
        return kvw[2 * pair:2 * pair + 2, kind, :, lanes(group)].reshape(256, 128)

    @pl.loop(0, 4)
    def _(i):
        group = lax.div(i, 2)
        pb = group * 4 + lax.rem(i, 2)
        raw = nt(kvn[0, :, lanes(group)], qs[pb])
        masked = bnoisy[...]
        st[pb, 1024:1152, :] = raw + jnp.concatenate([masked, masked], 1)

    def score(pair):
        @pl.loop(0, 8)
        def _(pb):
            group = lax.div(pb, 4)
            raw = nt(keys_of(pair, 0, group), qs[pb])
            masked = bias[lax.div(lax.rem(pb, 4), 2), pair * 256:(pair + 1) * 256, :]
            st[pb, pair * 256:(pair + 1) * 256, :] = raw + jnp.concatenate([masked, masked], 1)

    tick(1)
    kv_pass(1)
    kv_odd(1)
    score(0)
    tick(2)
    kv_pass(2)
    kv_odd(3)
    tick(3)
    score(1)
    kv_pass(3)
    kv_odd(5)
    tick(4)
    score(2)
    tick(5)
    kv_odd(7)
    score(3)
    tick(6)

    def turned(value):
        return value.astype(F32).T.astype(BF16)

    for group in range(2):
        for slot in range(9):
            part = slice(slot * 128, (slot + 1) * 128)
            width = slice(group * 128, (group + 1) * 128)
            for kind, target in ((0, kt), (1, vt)):
                rows = kvn[kind, :, width] if slot == 8 else kvw[slot, kind, :, width]
                target[group, :, part] = turned(rows)
    tick(7)

    def softmax(copy_id, low, high):
        count = 9 if copy_id == 0 else 8

        @pl.loop(low, high)
        def _(i):
            group = lax.div(i, 2)
            pair = lax.rem(i, 2)
            pb = group * 4 + copy_id * 2 + pair
            peak = jnp.max(st[pb, 0:128 * count, :], axis=0, keepdims=True)
            total = jnp.zeros((1, 256), F32)
            for block in range(count):
                part = slice(block * 128, (block + 1) * 128)
                weight = jnp.exp2((st[pb, part, :] - peak) * EXP2)
                total = total + jnp.sum(weight, axis=0, keepdims=True)
                pt[pb, part, :] = weight.astype(BF16)
            inverse = 1.0 / total
            lrow[pb] = jnp.broadcast_to(inverse, (8, 256))
            lcol[pb] = jnp.broadcast_to(inverse, (128, 256)).T
            result = nn(vt[group, :, 0:128 * count], pt[pb, 0:128 * count, :]) * inverse
            for half in range(2):
                head = group * 4 + pair * 2 + half
                block = result[:, half * 128:(half + 1) * 128].T.astype(BF16)
                att[copy_id * 128:(copy_id + 1) * 128, lanes(head)] = block

    softmax(0, 0, 2)
    tick(8)
    softmax(0, 2, 4)
    tick(9)
    softmax(1, 0, 2)
    tick(10)
    softmax(1, 2, 4)
    tick(11)
    get_g.wait()

    def plane(n):
        for i in range(2):
            @pl.when(core == 1 - i)
            def _():
                passed(i, n).wait_recv()

        dz = PLANES[n]
        zz = zs[dz]
        lines = [wbuf[zz, line].reshape(256, 1024) for line in range(2)]
        at = pl.multiple_of(zz * 512, 512)
        rows = gbuf[:, :, pl.ds(at, 512)].reshape(256, 512)
        for piece in range(4):
            part = slice(piece * 256, (piece + 1) * 256)
            term = nn(rows[:, 0:256], lines[0][:, part]) + nn(rows[:, 256:512], lines[1][:, part])
            if n == 0:
                gacc[:, part] = term
            else:
                gacc[:, part] += term
        where = lax.rem(zz, 4)
        mine = lax.div(zz, 4) == hd
        for line in range(2):
            part = slice(line * 256, (line + 1) * 256)
            value = nt(att[...], lines[line])

            @pl.when(mine)
            def _():
                ypart[where, :, part] = value

            @pl.when(jnp.logical_not(mine))
            def _():
                ysend[where, :, part] = value.astype(BF16)

        @pl.when(jnp.logical_not(mine))
        def _():
            remote(ysend.at[where], yrecv.at[where], es.at[where], er.at[where], dev_head).start()

    for n in range(8):
        if n < 4:
            tick(12 + n)
        plane(n)

    @pl.loop(0, 8)
    def _(pb):
        group = lax.div(pb, 4)
        copy_id = lax.div(lax.rem(pb, 4), 2)
        pair = lax.rem(pb, 2)
        rows = pl.ds(pl.multiple_of(copy_id * 128, 128), 128)
        for half in range(2):
            part = slice(half * 128, (half + 1) * 128)
            head = group * 4 + pair * 2 + half
            grad = gacc[rows, lanes(head)].astype(BF16).astype(F32)
            product = grad * att[rows, lanes(head)].astype(F32)
            delta = jnp.sum(product.T, axis=0, keepdims=True)
            dl[pb, :, part] = jnp.broadcast_to(delta, (8, 128)) * lrow[pb, :, part]
            gs[pb, part, :] = (grad * lcol[pb, part, :]).astype(BF16)

    def grads(keys, values, where, size, group, blocks):
        dk = jnp.zeros((size, 128), F32)
        dv = jnp.zeros((size, 128), F32)
        for b in blocks:
            pb = group * 4 + b
            flow = nt(values, gs[pb])
            weight = pt[pb, where:where + size, :]
            dscore = (weight.astype(F32) * (flow - dl[pb, 0:1, :])).astype(BF16)
            dst[pb, where:where + size, :] = dscore
            dv = dv + nn(weight, gs[pb])
            dk = dk + nn(dscore, qs[pb])
        return dk * SCALE, dv

    def send_odd(pair):
        src = stage.at[pair]

        @pl.when(core == 0)
        def _():
            if pair == 3:
                remote(src, ret.at[3], rs.at[3 + pair], rr.at[3], dev_seven).start()
            else:
                remote(src, col.at[pair], rs.at[3 + pair], rr.at[4 + pair], dev_pair).start()

        @pl.when(core == 1)
        def _():
            if pair == 0:
                remote(src, ret.at[3], rs.at[3 + pair], rr.at[3], dev_pair).start()
            else:
                remote(src, col.at[pair - 1], rs.at[3 + pair], rr.at[3 + pair], dev_pair).start()

    def collect(k):
        remote(col.at[k - 1], col.at[k - 1], rs.at[0], rr.at[3 + k], dev_pair).wait_recv()
        comb[k - 1] = (evens[k - 1] + col[k - 1].astype(F32)).astype(BF16)
        remote(comb.at[k - 1], ret.at[k - 1], rs.at[k - 1], rr.at[k - 1], earlier[k]).start()

    for pair in (3, 2, 1, 0):
        @pl.loop(0, 2)
        def _(group):
            dk, dv = grads(
                keys_of(pair, 0, group), keys_of(pair, 1, group), pair * 256, 256, group, range(4)
            )
            for kind, value in ((0, dk), (1, dv)):
                if pair == 0:
                    own[kind, :, lanes(group)] = value[0:128]
                else:
                    evens[pair - 1, kind, :, lanes(group)] = value[0:128]
                stage[pair, kind, :, lanes(group)] = value[128:256].astype(BF16)

        send_odd(pair)
        if pair in (0, 1):
            collect(pair + 2)

    @pl.loop(0, 2)
    def _(group):
        dk, dv = grads(
            kvn[0, :, lanes(group)], kvn[1, :, lanes(group)], 1024, 128, group, range(2)
        )
        dkvv[0, 0, :, lanes(group)] = dk
        dkvv[1, 0, :, lanes(group)] = dv

    def dqueries(copy_id):
        count = 1152 if copy_id == 0 else 1024

        @pl.loop(0, 4)
        def _(i):
            group = lax.div(i, 2)
            pair = lax.rem(i, 2)
            pb = group * 4 + copy_id * 2 + pair
            result = nn(kt[group, :, 0:count], dst[pb, 0:count, :]) * SCALE
            for half in range(2):
                head = group * 4 + pair * 2 + half
                dqv[copy_id, :, lanes(head)] = result[:, half * 128:(half + 1) * 128].T

        return fetch(dqv.at[copy_id], dq_hbm.at[copy_id], dsem.at[6 + copy_id])

    collect(1)
    dq0 = dqueries(0)
    dq1 = dqueries(1)

    for j in range(4):
        remote(ysend.at[j], yrecv.at[j], es.at[j], er.at[j], dev_head).wait_recv()
        part = slice(j * 512, (j + 1) * 512)
        total = ypart[j] + yrecv[j].astype(F32)
        for copy_id in range(2):
            yout[copy_id, :, part] = total[copy_id * 128:(copy_id + 1) * 128].astype(BF16)
    put_y = fetch(yout, out_hbm, dsem.at[0])

    for n in range(4):
        remote(ret.at[n], ret.at[n], rs.at[n], rr.at[n], dev_pair).wait_recv()
    for kind in range(2):
        total = own[kind]
        for n in range(4):
            total = total + ret[n, kind].astype(F32)
        dkvv[kind, 1] = total
    put_kv = fetch(dkvv, dkv_hbm, dsem.at[1])

    for copy in kv_far:
        copy.wait_send()
    w_first.wait_send()
    for k in (1, 2, 3):
        remote(kvw.at[2 * k], kvw.at[2 * k], ks.at[3 + k], kr.at[0], dev_pair).wait_send()
    kv_own.wait_send()
    for i in range(2):
        @pl.when(core == i)
        def _():
            for n, view in enumerate(sent[i]):
                remote(view(), view(), ws.at[n + 1], wr.at[0], dev_y).wait_send()
            for n in range(8):
                passed(i, n).wait_send()

    for j in range(4):
        remote(ysend.at[j], yrecv.at[j], es.at[j], er.at[j], dev_head).wait_send()
    for n in range(7):
        remote(stage.at[0], stage.at[0], rs.at[n], rr.at[0], dev_pair).wait_send()
    for copy in (dq0, dq1, put_y, put_kv):
        copy.wait()


def per_device(queries, keys_values, grad_layer, out_proj, doc_layout):
    vm = pltpu.VMEM
    dma = pltpu.SemaphoreType.DMA
    scratch = [
        vm((NZ, NY, NX, 2, 32, 1024), BF16),
        vm((8, 256, 128), BF16),
        vm((8, 2, 128, 256), BF16),
        vm((2, 128, 256), BF16),
        vm((2, 128, 4096), BF16),
        vm((3, 128), jnp.int32),
        vm((2, 1024, 128), F32),
        vm((128, 128), F32),
        vm((8, 1152, 256), F32),
        vm((8, 1152, 256), BF16),
        vm((8, 1152, 256), BF16),
        vm((2, 128, 1152), BF16),
        vm((2, 128, 1152), BF16),
        vm((256, 1024), BF16),
        vm((256, 1024), F32),
        vm((8, 8, 256), F32),
        vm((8, 256, 128), F32),
        vm((8, 256, 128), BF16),
        vm((8, 8, 256), F32),
        vm((4, 256, 512), F32),
        vm((4, 256, 512), BF16),
        vm((4, 256, 512), BF16),
        vm((2, 128, 2048), BF16),
        vm((4, 2, 128, 256), BF16),
        vm((3, 2, 128, 256), F32),
        vm((3, 2, 128, 256), BF16),
        vm((3, 2, 128, 256), BF16),
        vm((4, 2, 128, 256), BF16),
        vm((2, 128, 256), F32),
        vm((2, 128, 1024), F32),
        vm((2, 2, 128, 256), F32),
        dma((8,)), dma((8,)), dma((8,)), dma((48,)), dma((48,)),
        dma((8,)), dma((8,)), dma((4,)), dma((4,)), dma((8,)), dma((8,)),
    ]
    anywhere = pl.BlockSpec(memory_space=pl.ANY)
    return pl.pallas_call(
        kernel,
        out_shape=(
            jax.ShapeDtypeStruct((2, 128, 2048), BF16),
            jax.ShapeDtypeStruct((2, 128, 1024), F32),
            jax.ShapeDtypeStruct((2, 2, 128, 256), F32),
        ),
        in_specs=[anywhere] * 5,
        out_specs=(anywhere,) * 3,
        scratch_shapes=scratch,
        compiler_params=pltpu.CompilerParams(
            collective_id=0, has_side_effects=True, vmem_limit_bytes=62 * 1024 * 1024
        ),
    )(queries, keys_values, grad_layer, out_proj, doc_layout)


def solution(mesh):
    return jax.shard_map(
        per_device,
        mesh=mesh,
        in_specs=(
            P(None, "ctx", "head"),
            P(None, None, "ctx", "head"),
            P(None, "ctx", None),
            P("ctx", "head"),
            P(None, "ctx"),
        ),
        out_specs=(P(None, "ctx", "head"), P(None, "ctx", "head"), P(None, None, "ctx", "head")),
        check_vma=False,
    )
```

profile of v0, /device:TPU:71, one launch (start us, length us, event | category | flops | bytes accessed | tf_op | source)
XLA Modules:
  0.0 90.4 jit_solution(12786019512052590132)
XLA Ops:
  0.6 85.6 %shard_map.76 = (bf16[2,128,2048]{2,1,0:T(8,128)(2,1)}, f32[2,128,1024]{2,1,0:T(8,128)}, f32[2,2,128,256]{3,2,1,0:T(8,128)}) custom-call(bf16[2,128,1024]{2,1,0:T(8,128)(2,1)} %q_hbm.1, bf16[2,2,128,256]{3,2,1,0:T(8,128)(2,1)} %kv_hbm.1, bf16[2,128,4096]{2,1,0:T(8,128)(2,1)} %g_hbm.1, bf16[32,1024]{1,0:T(8,128)(2,1)} %w_hbm.1, s32[3,128]{1,0:T(4,128)} %lay_hbm.1), custom_call_target="tpu_custom_call" | custom-call | tf_op jit(solution)/shard_map/pallas_call | solution.py:597
  86.2 0.0 copy-start
  86.2 0.0 copy-start.1
  86.2 2.4 %copy.11 = bf16[2,128,2048]{2,1,0:T(8,128)(2,1)} copy(bf16[2,128,2048]{2,1,0:T(8,128)(2,1)} %get-tuple-element.6) | data formatting | bytes 2097152
  88.7 0.0 copy-done
  88.7 1.0 %copy.12 = f32[2,128,1024]{2,1,0:T(8,128)} copy(f32[2,128,1024]{2,1,0:T(8,128)S(1)} %copy-done) | data formatting | bytes 2097152
  89.6 0.0 copy-done.1
  89.6 0.8 copy.13
Async XLA Ops:
  86.2 2.4 %copy-start = (f32[2,128,1024]{2,1,0:T(8,128)S(1)}, f32[2,128,1024]{2,1,0:T(8,128)}, u32[]{:S(2)}) copy-start(f32[2,128,1024]{2,1,0:T(8,128)} %get-tuple-element.7) | copy-start | bytes 3145732
  86.2 3.4 %copy-start.1 = (f32[2,2,128,256]{3,2,1,0:T(8,128)S(1)}, f32[2,2,128,256]{3,2,1,0:T(8,128)}, u32[]{:S(2)}) copy-start(f32[2,2,128,256]{3,2,1,0:T(8,128)} %get-tuple-element.8) | copy-start | bytes 1572868
where the time goes:
time: 90.5 us; the launch traced here: 90.4 us
  Pallas kernels  85.6 us (95%)
  local copies, waits for them, and re-layouts  4.19 us (5%)
    pallas_call x1, Pallas kernels, per_device(): pl.pallas_call(kernel, out_shape=(jax.ShapeDtypeStruct((2, 128, 2048), BF...  85.6 us
    unnamed x7, local copies, waits for them, and re-layouts  4.19 us

commit v1 on v0

--- a/solution.py
+++ b/solution.py
@@ -31,9 +31,9 @@
 def kernel(
     q_hbm, kv_hbm, g_hbm, w_hbm, lay_hbm,
     out_hbm, dq_hbm, dkv_hbm,
-    wbuf, qs, kvw, kvn, gbuf, lay, bias, bnoisy, st, pt, dst, vt, kt,
+    wbuf, qs, kvw, kvp, kvn, gbuf, lay, bias, bnoisy, st, pt, dst, vt, kt,
     att, gacc, lrow, lcol, gs, dl, ypart, ysend, yrecv, yout,
-    stage, evens, col, comb, ret, own, dqv, dkvv,
+    stage, evens, col, comb, ret, back, retp, own, dqv, dkvv,
     dsem, ks, kr, ws, wr, pps, ppr, es, er, rs, rr,
 ):
     ctx = lax.axis_index("ctx")
@@ -53,9 +53,11 @@
     dev_z = [(place(zs[1], yh, x), hd), (place(zs[7], yh, x), hd)]
     dev_pair = (ctx + 1 - 2 * core, hd)
     dev_head = (ctx, 1 - hd)
-    later = [(lax.rem(ctx + 2 * k, 128), hd) for k in range(4)]
-    earlier = [(lax.rem(ctx + 128 - 2 * k, 128), hd) for k in range(4)]
-    dev_seven = (lax.rem(ctx + 121 + 14 * core, 128), hd)
+    line = [(place(z, yh, xs[k]), hd) for k in range(NX)]
+    dev_after = (lax.rem(ctx + 8, 128), hd)
+    dev_prior = (lax.rem(ctx + 126, 128), hd)
+    dev_follow = (lax.rem(ctx + 2, 128), hd)
+    dev_before = (lax.rem(ctx + 120, 128), hd)
 
     def remote(src, dst_ref, send, recv, device):
         return pltpu.make_async_remote_copy(
@@ -83,32 +85,41 @@
     get_g = fetch(g_hbm, gbuf, dsem.at[5])
 
     barrier = pltpu.get_barrier_semaphore()
-    meet = [dev_y, *dev_x, *dev_z, dev_pair, dev_head, *later[1:], *earlier[1:], dev_seven]
+    planar = [(place(z, 1 - yh, xs[k]), hd) for k in range(NX)]
+    meet = [*planar, *line[1:], *dev_z, dev_pair, dev_head, dev_after, dev_before, dev_prior, dev_follow]
     for device in meet:
         pl.semaphore_signal(barrier, inc=1, device_id=device, device_id_type=MESH)
     pl.semaphore_wait(barrier, len(meet))
 
     own_kv = kv_hbm.at[:, 1]
-    kv_far = [remote(own_kv, kvw.at[2 * k], ks.at[k], kr.at[2 * k], later[k]) for k in (1, 2, 3)]
-    kv_seven = remote(own_kv, kvw.at[7], ks.at[0], kr.at[7], dev_seven)
-    kv_own = remote(own_kv, kvw.at[1], ks.at[0], kr.at[1], dev_pair)
-
-    w_first = remote(w_hbm, wbuf.at[z, yh, x, core], ws.at[0], wr.at[0], dev_y)
-    w_first.start()
-
-    @pl.when(core == 0)
-    def _():
-        kv_own.start()
-
-    for copy in kv_far:
-        copy.start()
-
-    @pl.when(core == 1)
-    def _():
-        kv_seven.start()
+    kv_next = remote(own_kv, kvp, ks.at[7], kr.at[0], dev_after)
+
+    def kv_start():
+        kv_next.start()
+
+        @pl.when(core == 0)
+        def _():
+            remote(own_kv, kvw.at[1], ks.at[0], kr.at[1], dev_pair).start()
+
+    def kv_line():
+        for k in (1, 2, 3):
+            @pl.when(x + k < NX)
+            def _():
+                remote(own_kv, kvw.at[2 * k], ks.at[k], kr.at[2 * k], line[k]).start()
+
+    def kv_before():
+        kv_next.wait_recv()
+        for k in (1, 2, 3):
+            @pl.when(x + k >= NX)
+            def _():
+                remote(kvp, kvw.at[2 * k], ks.at[k], kr.at[2 * k], line[k]).start()
+
+        @pl.when(core == 1)
+        def _():
+            remote(kvp, kvw.at[7], ks.at[0], kr.at[7], dev_pair).start()
 
     def kv_pass(k):
-        kv_far[k - 1].wait_recv()
+        remote(kvp, kvw.at[2 * k], ks.at[k], kr.at[2 * k], line[k]).wait_recv()
 
         @pl.when(core == 0)
         def _():
@@ -127,10 +138,11 @@
 
     sent = ([], [])
 
-    def send_w(core_id, view, device, recv):
-        n = len(sent[core_id]) + 1
-        src = view()
-        remote(src, src, ws.at[n], wr.at[recv], device).start()
+    def send_w(core_id, view, device, recv, source=None):
+        n = len(sent[core_id])
+        target = view()
+        src = target if source is None else source
+        remote(src, target, ws.at[n], wr.at[recv], device).start()
         sent[core_id].append(view)
 
     def wait_w(src, recv):
@@ -143,137 +155,185 @@
     def pass_plane(core_id, n):
         passed(core_id, n).start()
 
-    def sub0(dz, dx):
-        return wbuf.at[zs[dz], :, xs[dx], 0]
-
-    def zrecv0(way, hop, s):
-        return 5 + (way * 4 + hop - 1) * 4 + s
+    low = lax.rem(lax.div(x, 2) * 2, NX)
+    high = lax.rem(low + 2, NX)
+    mate = low + 1 - lax.rem(x, 2)
+    across = 1 - yh
+
+    def sub0(dz, sub):
+        row = yh if sub < 2 else across
+        return wbuf.at[zs[dz], row, pl.ds(low if sub % 2 == 0 else high, 2), 0]
+
+    def zrecv0(way, hop, sub):
+        return 6 + (way * 4 + hop - 1) * 4 + sub
+
+    def away(way, hop):
+        return (8 - hop) % 8 if way == 0 else hop
+
+    def near(k):
+        row = yh if k < NX else across
+        return wbuf.at[z, row, xs[k % NX], 0]
 
     def ticks0():
-        def first():
+        def start(*steps):
+            for k in steps:
+                device = line[k] if k < NX else (place(z, across, xs[k % NX]), hd)
+                send_w(0, lambda: near(0), device, 38 + k, w_hbm)
+
+        def start_z():
+            for way in range(2):
+                send_w(0, lambda: near(0), dev_z[way], zrecv0(way, 1, 0), w_hbm)
+
+        def shard_at(row, col):
+            return wbuf.at[z, row, col, 0]
+
+        def arrive(k):
+            row = yh if k < NX else across
+            wait_w(wbuf.at[z, row, xs[(NX - k % NX) % NX], 0], 38 + k)
+
+        def all_near():
+            for k in range(2, 8):
+                if k != 3:
+                    arrive(k)
+            for sub in range(1, 4):
+                zhop(sub, 0)
+
+        def mate_first():
             get_w.wait()
-            w_first.wait_recv()
+            for k in (1, 3):
+                arrive(k)
             for way in range(2):
-                send_w(0, lambda: sub0(0, 0), dev_x[way], 1 + way)
+                send_w(0, lambda: shard_at(yh, mate), dev_z[way], zrecv0(way, 1, 0))
+
+        def zhop(sub, hop):
             for way in range(2):
-                send_w(0, lambda: sub0(0, 0), dev_z[way], zrecv0(way, 1, 0))
-
-        def second():
-            for way, (dx, half) in enumerate(((3, 0), (1, 1))):
-                wait_w(sub0(0, dx), 1 + way)
-                send_w(0, lambda dx=dx, half=half: wbuf.at[z, half, xs[dx], 0], dev_x[way], 3 + way)
-                for zway in range(2):
-                    send_w(0, lambda dx=dx: sub0(0, dx), dev_z[zway], zrecv0(zway, 1, 1 + way))
-
-        def third():
-            for way in range(2):
-                wait_w(wbuf.at[z, way, xs[2], 0], 3 + way)
-            for way in range(2):
-                send_w(0, lambda: sub0(0, 2), dev_z[way], zrecv0(way, 1, 3))
-            pass_plane(0, 0)
-
-        def hop_step(hop, s):
-            for way in range(2):
-                dz = (8 - hop) if way == 0 else hop
-                half = (0, 1) if way == 0 else (2, 3)
-                if hop == 4 and s not in half:
-                    continue
-                wait_w(sub0(dz, SUBS[s]), zrecv0(way, hop, s))
-                if hop < 3 or (hop == 3 and s in half):
-                    send_w(0, lambda dz=dz: sub0(dz, SUBS[s]), dev_z[way], zrecv0(way, hop + 1, s))
-            if s == 3 and hop < 4:
-                pass_plane(0, 2 * hop - 1)
-                pass_plane(0, 2 * hop)
-            if s == 3 and hop == 4:
-                pass_plane(0, 7)
-
-        yield first
-        yield second
-        yield third
-        for hop in range(1, 4):
-            for s in range(4):
-                yield functools.partial(hop_step, hop, s)
-
-        def last():
-            for s in range(4):
-                hop_step(4, s)
-
-        yield last
+                half = sub < 2 if way == 0 else sub >= 2
+                if hop > 0:
+                    if hop == 4 and not half:
+                        continue
+                    wait_w(sub0(away(way, hop), sub), zrecv0(way, hop, sub))
+                if hop < 3 or (hop == 3 and half):
+                    send_w(0, lambda way=way: sub0(away(way, hop), sub), dev_z[way],
+                           zrecv0(way, hop + 1, sub))
+
+        def give(*planes):
+            for n in planes:
+                pass_plane(0, n)
+
+        plan = [
+            [(start_z,), (start, 1, 3)],
+            [(mate_first,)],
+            [(all_near,)],
+            [(zhop, 0, 1)],
+            [(zhop, 1, 1), (zhop, 2, 1), (give, 0)],
+            [(zhop, 3, 1), (zhop, 0, 2)],
+            [(zhop, 1, 2), (give, 1, 2)],
+            [(zhop, 2, 2)],
+            [(zhop, 3, 2)],
+            [(zhop, 0, 3), (zhop, 1, 3), (give, 3, 4)],
+            [(zhop, 2, 3)],
+            [(zhop, 3, 3)],
+            [(give, 5, 6), (zhop, 0, 4), (zhop, 1, 4)],
+            [],
+            [(zhop, 2, 4), (zhop, 3, 4), (give, 7)],
+            [], [], [],
+            [(start, 4, 2, 5, 7, 6)],
+        ]
+        return [functools.partial(run, steps) for steps in plan]
+
+    def run(steps):
+        for step, *values in steps:
+            step(*values)
 
     def ticks1():
-        def zblock(dz):
-            return wbuf.at[zs[dz], :, x, 1]
-
-        def xrecv(n, kind, way):
-            return 9 + n * 4 + kind * 2 + way
-
-        def x1(n):
-            for way in range(2):
-                send_w(1, lambda: zblock(PLANES[n]), dev_x[way], xrecv(n, 0, way))
-
-        def x2(n):
-            dz = PLANES[n]
-            for way, (dx, half) in enumerate(((3, 0), (1, 1))):
-                wait_w(wbuf.at[zs[dz], :, xs[dx], 1], xrecv(n, 0, way))
-                send_w(1, lambda dx=dx, half=half: wbuf.at[zs[dz], half, xs[dx], 1], dev_x[way], xrecv(n, 1, way))
-
-        def done(n):
-            for way in range(2):
-                wait_w(wbuf.at[zs[PLANES[n]], way, xs[2], 1], xrecv(n, 1, way))
-            pass_plane(1, n)
+        def shard(n, other):
+            return wbuf.at[zs[PLANES[n]], across if other else yh, x, 1]
+
+        def beside(n, other, dx):
+            return wbuf.at[zs[PLANES[n]], across if other else yh, xs[dx], 1]
+
+        def xrecv(n, other, way):
+            return 16 + n * 6 + other * 3 + way
+
+        def yout(*planes):
+            for n in planes:
+                local = {"source": w_hbm} if n == 0 else {}
+                send_w(1, lambda n=n: shard(n, 0), dev_y, 8 + n, **local)
+
+        def xout(*planes):
+            for n in planes:
+                local = {"source": w_hbm} if n == 0 else {}
+                for way in range(2):
+                    send_w(1, lambda n=n: shard(n, 0), dev_x[way], xrecv(n, 0, way), **local)
+
+        def turn(*planes):
+            for n in planes:
+                wait_w(shard(n, 1), 8 + n)
+                for way in range(2):
+                    send_w(1, lambda n=n: shard(n, 1), dev_x[way], xrecv(n, 1, way))
+
+        def onward(other, *planes):
+            for n in planes:
+                for way, dx in enumerate((3, 1)):
+                    wait_w(beside(n, other, dx), xrecv(n, other, way))
+                dx = 1 if other else 3
+                send_w(1, lambda n=n: beside(n, other, dx), dev_x[other], xrecv(n, other, 2))
+
+        def give(*planes):
+            for n in planes:
+                for other in range(2):
+                    wait_w(beside(n, other, 2), xrecv(n, other, 2))
+                pass_plane(1, n)
+
+        def half(dz, way):
+            return wbuf.at[zs[dz], yh, x, 1, pl.ds(16 * way, 16)]
 
         def zhop(hop):
             for way in range(2):
-                dz = (8 - hop) if way == 0 else hop
+                dz = away(way, hop)
                 if hop == 4:
-                    wait_w(wbuf.at[zs[4], way, x, 1], 1 + way * 4 + 3)
+                    wait_w(half(4, way), way * 4 + 3)
                     continue
-                wait_w(zblock(dz), 1 + way * 4 + hop - 1)
+                if hop > 0:
+                    wait_w(wbuf.at[zs[dz], yh, x, 1], way * 4 + hop - 1)
 
                 def view(dz=dz, way=way):
-                    return zblock(dz) if hop < 3 else wbuf.at[zs[dz], way, x, 1]
-
-                send_w(1, view, dev_z[way], 1 + way * 4 + hop)
-
-        def first():
-            get_w.wait()
-            w_first.wait_recv()
-            for way in range(2):
-                send_w(1, lambda: zblock(0), dev_z[way], 1 + way * 4)
-            x1(0)
+                    return half(dz, way) if hop == 3 else wbuf.at[zs[dz], yh, x, 1]
+
+                local = {"source": w_hbm} if hop == 0 else {}
+                send_w(1, view, dev_z[way], way * 4 + hop, **local)
 
         plan = [
-            [(zhop, 1), (x1, 1), (x1, 2)],
-            [(x2, 0)],
-            [(zhop, 2), (x1, 3), (x1, 4)],
-            [(x2, 1), (x2, 2), (done, 0)],
-            [(zhop, 3), (x1, 5), (x1, 6)],
-            [(x2, 3)],
-            [(done, 1), (done, 2), (zhop, 4), (x1, 7)],
-            [(x2, 4)],
-            [(x2, 5)],
-            [(done, 3), (done, 4), (x2, 6)],
-            [(x2, 7)],
-            [(done, 5)],
-            [(done, 6)],
-            [(done, 7)],
+            [(zhop, 0), (yout, 0)],
+            [(zhop, 1), (yout, 1, 2)],
+            [(zhop, 2), (yout, 3, 4), (xout, 0, 1, 2)],
+            [(zhop, 3), (yout, 5, 6), (turn, 0, 1, 2), (xout, 3, 4)],
+            [(zhop, 4), (yout, 7), (onward, 0, 0, 1, 2), (turn, 3, 4), (xout, 5, 6), (onward, 1, 0, 1, 2)],
+            [(onward, 0, 3, 4), (turn, 5, 6), (xout, 7), (get_w.wait,), (give, 0)],
+            [(onward, 1, 3, 4), (turn, 7), (give, 1, 2)],
+            [(onward, 0, 5, 6)],
+            [(onward, 1, 5, 6)],
+            [(onward, 0, 7), (give, 3, 4)],
+            [(onward, 1, 7)],
             [],
+            [(give, 5, 6)],
+            [],
+            [(give, 7)],
+            [], [], [], [],
         ]
-
-        def run(steps):
-            for step, value in steps:
-                step(value)
-
-        yield first
-        for steps in plan:
-            yield functools.partial(run, steps)
-
-    zero_ticks, one_ticks = list(ticks0()), list(ticks1())
-    assert len(zero_ticks) == len(one_ticks) == 16
+        return [functools.partial(run, steps) for steps in plan]
+
+    zero_ticks, one_ticks = ticks0(), ticks1()
+    assert len(zero_ticks) == len(one_ticks) == 19
 
     def tick(n):
         pl.when(core == 0)(zero_ticks[n])
         pl.when(core == 1)(one_ticks[n])
+
+    tick(0)
+    kv_start()
+    tick(18)
+    kv_line()
 
     get_lay.wait()
     first = ctx * 128
@@ -290,7 +350,6 @@
         bias[0, slot * 128:(slot + 1) * 128, :] = far
         bias[1, slot * 128:(slot + 1) * 128, :] = far
 
-    tick(0)
     pltpu.make_async_copy(qs, qs, dsem.at[4]).wait()
     get_kv.wait()
     get_kn.wait()
@@ -310,7 +369,7 @@
         st[pb, 1024:1152, :] = raw + jnp.concatenate([masked, masked], 1)
 
     def score(pair):
-        @pl.loop(0, 8)
+        @pl.loop(0, 8, unroll=4)
         def _(pb):
             group = lax.div(pb, 4)
             raw = nt(keys_of(pair, 0, group), qs[pb])
@@ -318,22 +377,22 @@
             st[pb, pair * 256:(pair + 1) * 256, :] = raw + jnp.concatenate([masked, masked], 1)
 
     tick(1)
+    kv_before()
+    tick(2)
+    tick(3)
     kv_pass(1)
     kv_odd(1)
     score(0)
-    tick(2)
     kv_pass(2)
     kv_odd(3)
-    tick(3)
     score(1)
     kv_pass(3)
+    tick(4)
     kv_odd(5)
-    tick(4)
     score(2)
-    tick(5)
     kv_odd(7)
     score(3)
-    tick(6)
+    tick(5)
 
     def turned(value):
         return value.astype(F32).T.astype(BF16)
@@ -345,12 +404,12 @@
             for kind, target in ((0, kt), (1, vt)):
                 rows = kvn[kind, :, width] if slot == 8 else kvw[slot, kind, :, width]
                 target[group, :, part] = turned(rows)
-    tick(7)
+
 
     def softmax(copy_id, low, high):
         count = 9 if copy_id == 0 else 8
 
-        @pl.loop(low, high)
+        @pl.loop(low, high, unroll=2)
         def _(i):
             group = lax.div(i, 2)
             pair = lax.rem(i, 2)
@@ -371,14 +430,11 @@
                 block = result[:, half * 128:(half + 1) * 128].T.astype(BF16)
                 att[copy_id * 128:(copy_id + 1) * 128, lanes(head)] = block
 
+    softmax(1, 0, 2)
+    softmax(1, 2, 4)
+    tick(6)
     softmax(0, 0, 2)
-    tick(8)
     softmax(0, 2, 4)
-    tick(9)
-    softmax(1, 0, 2)
-    tick(10)
-    softmax(1, 2, 4)
-    tick(11)
     get_g.wait()
 
     def plane(n):
@@ -391,6 +447,15 @@
         zz = zs[dz]
         lines = [wbuf[zz, line].reshape(256, 1024) for line in range(2)]
         at = pl.multiple_of(zz * 512, 512)
+        where = lax.rem(zz, 4)
+
+        @pl.when(lax.div(zz, 4) != hd)
+        def _():
+            for line in range(2):
+                value = nt(att[...], wbuf[zz, line].reshape(256, 1024))
+                ysend[where, :, line * 256:(line + 1) * 256] = value.astype(BF16)
+            remote(ysend.at[where], yrecv.at[where], es.at[where], er.at[where], dev_head).start()
+
         rows = gbuf[:, :, pl.ds(at, 512)].reshape(256, 512)
         for piece in range(4):
             part = slice(piece * 256, (piece + 1) * 256)
@@ -399,30 +464,12 @@
                 gacc[:, part] = term
             else:
                 gacc[:, part] += term
-        where = lax.rem(zz, 4)
-        mine = lax.div(zz, 4) == hd
-        for line in range(2):
-            part = slice(line * 256, (line + 1) * 256)
-            value = nt(att[...], lines[line])
-
-            @pl.when(mine)
-            def _():
-                ypart[where, :, part] = value
-
-            @pl.when(jnp.logical_not(mine))
-            def _():
-                ysend[where, :, part] = value.astype(BF16)
-
-        @pl.when(jnp.logical_not(mine))
-        def _():
-            remote(ysend.at[where], yrecv.at[where], es.at[where], er.at[where], dev_head).start()
 
     for n in range(8):
-        if n < 4:
-            tick(12 + n)
+        tick(7 + n)
         plane(n)
 
-    @pl.loop(0, 8)
+    @pl.loop(0, 8, unroll=2)
     def _(pb):
         group = lax.div(pb, 4)
         copy_id = lax.div(lax.rem(pb, 4), 2)
@@ -456,7 +503,7 @@
         @pl.when(core == 0)
         def _():
             if pair == 3:
-                remote(src, ret.at[3], rs.at[3 + pair], rr.at[3], dev_seven).start()
+                remote(src, ret.at[3], rs.at[3 + pair], rr.at[3], dev_pair).start()
             else:
                 remote(src, col.at[pair], rs.at[3 + pair], rr.at[4 + pair], dev_pair).start()
 
@@ -470,10 +517,10 @@
     def collect(k):
         remote(col.at[k - 1], col.at[k - 1], rs.at[0], rr.at[3 + k], dev_pair).wait_recv()
         comb[k - 1] = (evens[k - 1] + col[k - 1].astype(F32)).astype(BF16)
-        remote(comb.at[k - 1], ret.at[k - 1], rs.at[k - 1], rr.at[k - 1], earlier[k]).start()
+        remote(comb.at[k - 1], ret.at[k - 1], rs.at[k - 1], rr.at[k - 1], line[NX - k] if k > 1 else dev_prior).start()
 
     for pair in (3, 2, 1, 0):
-        @pl.loop(0, 2)
+        @pl.loop(0, 2, unroll=2)
         def _(group):
             dk, dv = grads(
                 keys_of(pair, 0, group), keys_of(pair, 1, group), pair * 256, 256, group, range(4)
@@ -486,8 +533,14 @@
                 stage[pair, kind, :, lanes(group)] = value[128:256].astype(BF16)
 
         send_odd(pair)
-        if pair in (0, 1):
-            collect(pair + 2)
+        if pair < 3:
+            @pl.when(core == 0)
+            def _():
+                collect(pair + 1)
+        if pair < 2:
+            @pl.when(core == 1)
+            def _():
+                collect(pair + 2)
 
     @pl.loop(0, 2)
     def _(group):
@@ -500,7 +553,7 @@
     def dqueries(copy_id):
         count = 1152 if copy_id == 0 else 1024
 
-        @pl.loop(0, 4)
+        @pl.loop(0, 4, unroll=2)
         def _(i):
             group = lax.div(i, 2)
             pair = lax.rem(i, 2)
@@ -512,44 +565,67 @@
 
         return fetch(dqv.at[copy_id], dq_hbm.at[copy_id], dsem.at[6 + copy_id])
 
-    collect(1)
+    pl.when(core == 1)(functools.partial(collect, 1))
     dq0 = dqueries(0)
+
+    def line_sums():
+        for n in (2, 1, 3):
+            remote(ret.at[n], ret.at[n], rs.at[n], rr.at[n], dev_pair).wait_recv()
+        for kind in range(2):
+            mine, other = own[kind], jnp.zeros((128, 256), F32)
+            for n in (1, 2, 3):
+                here = core == 0 if n == 3 else x + n + 1 < NX
+                value = ret[n, kind].astype(F32)
+                mine = mine + jnp.where(here, value, 0.0)
+                other = other + jnp.where(here, 0.0, value)
+            own[kind] = mine
+            back[kind] = other.astype(BF16)
+        remote(back, retp, rs.at[7], rr.at[7], dev_before).start()
+
+    line_sums()
     dq1 = dqueries(1)
 
+    def mine(j):
+        for line_id in range(2):
+            part = slice(line_id * 256, (line_id + 1) * 256)
+            ypart[j, :, part] = nt(att[...], wbuf[hd * 4 + j, line_id].reshape(256, 1024))
+
     for j in range(4):
+        mine(j)
+
+    def finish(j):
         remote(ysend.at[j], yrecv.at[j], es.at[j], er.at[j], dev_head).wait_recv()
         part = slice(j * 512, (j + 1) * 512)
         total = ypart[j] + yrecv[j].astype(F32)
         for copy_id in range(2):
             yout[copy_id, :, part] = total[copy_id * 128:(copy_id + 1) * 128].astype(BF16)
+
+    for j in range(4):
+        finish(j)
     put_y = fetch(yout, out_hbm, dsem.at[0])
 
-    for n in range(4):
-        remote(ret.at[n], ret.at[n], rs.at[n], rr.at[n], dev_pair).wait_recv()
-    for kind in range(2):
-        total = own[kind]
-        for n in range(4):
-            total = total + ret[n, kind].astype(F32)
-        dkvv[kind, 1] = total
+    def last_sum():
+        remote(ret.at[0], ret.at[0], rs.at[0], rr.at[0], dev_pair).wait_recv()
+        remote(back, retp, rs.at[7], rr.at[7], dev_before).wait_recv()
+        for kind in range(2):
+            dkvv[kind, 1] = own[kind] + ret[0, kind].astype(F32) + retp[kind].astype(F32)
+
+    last_sum()
     put_kv = fetch(dkvv, dkv_hbm, dsem.at[1])
 
-    for copy in kv_far:
-        copy.wait_send()
-    w_first.wait_send()
-    for k in (1, 2, 3):
-        remote(kvw.at[2 * k], kvw.at[2 * k], ks.at[3 + k], kr.at[0], dev_pair).wait_send()
-    kv_own.wait_send()
+    for n in range(8):
+        remote(own_kv, kvp, ks.at[n], kr.at[0], dev_after).wait_send()
     for i in range(2):
         @pl.when(core == i)
         def _():
             for n, view in enumerate(sent[i]):
-                remote(view(), view(), ws.at[n + 1], wr.at[0], dev_y).wait_send()
+                remote(view(), view(), ws.at[n], wr.at[0], dev_y).wait_send()
             for n in range(8):
                 passed(i, n).wait_send()
 
     for j in range(4):
         remote(ysend.at[j], yrecv.at[j], es.at[j], er.at[j], dev_head).wait_send()
-    for n in range(7):
+    for n in range(8):
         remote(stage.at[0], stage.at[0], rs.at[n], rr.at[0], dev_pair).wait_send()
     for copy in (dq0, dq1, put_y, put_kv):
         copy.wait()
@@ -562,6 +638,7 @@
         vm((NZ, NY, NX, 2, 32, 1024), BF16),
         vm((8, 256, 128), BF16),
         vm((8, 2, 128, 256), BF16),
+        vm((2, 128, 256), BF16),
         vm((2, 128, 256), BF16),
         vm((2, 128, 4096), BF16),
         vm((3, 128), jnp.int32),
@@ -587,10 +664,12 @@
         vm((3, 2, 128, 256), BF16),
         vm((3, 2, 128, 256), BF16),
         vm((4, 2, 128, 256), BF16),
+        vm((2, 128, 256), BF16),
+        vm((2, 128, 256), BF16),
         vm((2, 128, 256), F32),
         vm((2, 128, 1024), F32),
         vm((2, 2, 128, 256), F32),
-        dma((8,)), dma((8,)), dma((8,)), dma((48,)), dma((48,)),
+        dma((8,)), dma((8,)), dma((8,)), dma((72,)), dma((72,)),
         dma((8,)), dma((8,)), dma((4,)), dma((4,)), dma((8,)), dma((8,)),
     ]
     anywhere = pl.BlockSpec(memory_space=pl.ANY)

time: 90.5 us -> 75.5 us (0.83)
  the two profiles are of different devices: /device:TPU:71 before, /device:TPU:7 now
where the time goes in v1:
time: 75.5 us; the launch traced here: 75.3 us
  Pallas kernels  70.5 us (93%)
  local copies, waits for them, and re-layouts  4.19 us (6%)
    pallas_call x1, Pallas kernels, per_device(): pl.pallas_call(kernel, out_shape=(jax.ShapeDtypeStruct((2, 128, 2048), BF...  70.5 us
    unnamed x7, local copies, waits for them, and re-layouts  4.19 us

profile of v1, /device:TPU:7, one launch (start us, length us, event | category | flops | bytes accessed | tf_op | source)
XLA Modules:
  0.0 75.3 jit_solution(6975811019339371120)
XLA Ops:
  0.6 70.5 %shard_map.76 = (bf16[2,128,2048]{2,1,0:T(8,128)(2,1)}, f32[2,128,1024]{2,1,0:T(8,128)}, f32[2,2,128,256]{3,2,1,0:T(8,128)}) custom-call(bf16[2,128,1024]{2,1,0:T(8,128)(2,1)} %q_hbm.1, bf16[2,2,128,256]{3,2,1,0:T(8,128)(2,1)} %kv_hbm.1, bf16[2,128,4096]{2,1,0:T(8,128)(2,1)} %g_hbm.1, bf16[32,1024]{1,0:T(8,128)(2,1)} %w_hbm.1, s32[3,128]{1,0:T(4,128)} %lay_hbm.1), custom_call_target="tpu_custom_call" | custom-call | tf_op jit(solution)/shard_map/pallas_call | solution.py:676
  71.1 0.0 copy-start
  71.1 0.0 copy-start.1
  71.2 2.4 %copy.11 = bf16[2,128,2048]{2,1,0:T(8,128)(2,1)} copy(bf16[2,128,2048]{2,1,0:T(8,128)(2,1)} %get-tuple-element.6) | data formatting | bytes 2097152
  73.6 0.0 copy-done
  73.6 1.0 %copy.12 = f32[2,128,1024]{2,1,0:T(8,128)} copy(f32[2,128,1024]{2,1,0:T(8,128)S(1)} %copy-done) | data formatting | bytes 2097152
  74.5 0.0 copy-done.1
  74.5 0.8 %copy.13 = f32[2,2,128,256]{3,2,1,0:T(8,128)} copy(f32[2,2,128,256]{3,2,1,0:T(8,128)S(1)} %copy-done.1) | data formatting | bytes 1048576
Async XLA Ops:
  71.1 2.4 %copy-start = (f32[2,128,1024]{2,1,0:T(8,128)S(1)}, f32[2,128,1024]{2,1,0:T(8,128)}, u32[]{:S(2)}) copy-start(f32[2,128,1024]{2,1,0:T(8,128)} %get-tuple-element.7) | copy-start | bytes 3145732
  71.1 3.4 %copy-start.1 = (f32[2,2,128,256]{3,2,1,0:T(8,128)S(1)}, f32[2,2,128,256]{3,2,1,0:T(8,128)}, u32[]{:S(2)}) copy-start(f32[2,2,128,256]{3,2,1,0:T(8,128)} %get-tuple-element.8) | copy-start | bytes 1572868

commit v2 on v1

--- a/solution.py
+++ b/solution.py
@@ -30,10 +30,10 @@
 
 def kernel(
     q_hbm, kv_hbm, g_hbm, w_hbm, lay_hbm,
-    out_hbm, dq_hbm, dkv_hbm,
+    yout, dqv, dkvv,
     wbuf, qs, kvw, kvp, kvn, gbuf, lay, bias, bnoisy, st, pt, dst, vt, kt,
-    att, gacc, lrow, lcol, gs, dl, ypart, ysend, yrecv, yout,
-    stage, evens, col, comb, ret, back, retp, own, dqv, dkvv,
+    att, gacc, lrow, lcol, gs, dl, ypart, ysend, yrecv,
+    stage, evens, col, comb, ret, back, retp, own,
     dsem, ks, kr, ws, wr, pps, ppr, es, er, rs, rr,
 ):
     ctx = lax.axis_index("ctx")
@@ -55,8 +55,6 @@
     dev_head = (ctx, 1 - hd)
     line = [(place(z, yh, xs[k]), hd) for k in range(NX)]
     dev_after = (lax.rem(ctx + 8, 128), hd)
-    dev_prior = (lax.rem(ctx + 126, 128), hd)
-    dev_follow = (lax.rem(ctx + 2, 128), hd)
     dev_before = (lax.rem(ctx + 120, 128), hd)
 
     def remote(src, dst_ref, send, recv, device):
@@ -86,7 +84,7 @@
 
     barrier = pltpu.get_barrier_semaphore()
     planar = [(place(z, 1 - yh, xs[k]), hd) for k in range(NX)]
-    meet = [*planar, *line[1:], *dev_z, dev_pair, dev_head, dev_after, dev_before, dev_prior, dev_follow]
+    meet = [*planar, *line[1:], *dev_z, dev_pair, dev_head, dev_after, dev_before]
     for device in meet:
         pl.semaphore_signal(barrier, inc=1, device_id=device, device_id_type=MESH)
     pl.semaphore_wait(barrier, len(meet))
@@ -517,7 +515,7 @@
     def collect(k):
         remote(col.at[k - 1], col.at[k - 1], rs.at[0], rr.at[3 + k], dev_pair).wait_recv()
         comb[k - 1] = (evens[k - 1] + col[k - 1].astype(F32)).astype(BF16)
-        remote(comb.at[k - 1], ret.at[k - 1], rs.at[k - 1], rr.at[k - 1], line[NX - k] if k > 1 else dev_prior).start()
+        remote(comb.at[k - 1], ret.at[k - 1], rs.at[k - 1], rr.at[k - 1], line[NX - k]).start()
 
     for pair in (3, 2, 1, 0):
         @pl.loop(0, 2, unroll=2)
@@ -563,17 +561,16 @@
                 head = group * 4 + pair * 2 + half
                 dqv[copy_id, :, lanes(head)] = result[:, half * 128:(half + 1) * 128].T
 
-        return fetch(dqv.at[copy_id], dq_hbm.at[copy_id], dsem.at[6 + copy_id])
 
     pl.when(core == 1)(functools.partial(collect, 1))
-    dq0 = dqueries(0)
+    dqueries(0)
 
     def line_sums():
-        for n in (2, 1, 3):
+        for n in (2, 1, 0, 3):
             remote(ret.at[n], ret.at[n], rs.at[n], rr.at[n], dev_pair).wait_recv()
         for kind in range(2):
             mine, other = own[kind], jnp.zeros((128, 256), F32)
-            for n in (1, 2, 3):
+            for n in range(4):
                 here = core == 0 if n == 3 else x + n + 1 < NX
                 value = ret[n, kind].astype(F32)
                 mine = mine + jnp.where(here, value, 0.0)
@@ -583,7 +580,7 @@
         remote(back, retp, rs.at[7], rr.at[7], dev_before).start()
 
     line_sums()
-    dq1 = dqueries(1)
+    dqueries(1)
 
     def mine(j):
         for line_id in range(2):
@@ -602,16 +599,13 @@
 
     for j in range(4):
         finish(j)
-    put_y = fetch(yout, out_hbm, dsem.at[0])
 
     def last_sum():
-        remote(ret.at[0], ret.at[0], rs.at[0], rr.at[0], dev_pair).wait_recv()
         remote(back, retp, rs.at[7], rr.at[7], dev_before).wait_recv()
         for kind in range(2):
-            dkvv[kind, 1] = own[kind] + ret[0, kind].astype(F32) + retp[kind].astype(F32)
+            dkvv[kind, 1] = own[kind] + retp[kind].astype(F32)
 
     last_sum()
-    put_kv = fetch(dkvv, dkv_hbm, dsem.at[1])
 
     for n in range(8):
         remote(own_kv, kvp, ks.at[n], kr.at[0], dev_after).wait_send()
@@ -627,8 +621,6 @@
         remote(ysend.at[j], yrecv.at[j], es.at[j], er.at[j], dev_head).wait_send()
     for n in range(8):
         remote(stage.at[0], stage.at[0], rs.at[n], rr.at[0], dev_pair).wait_send()
-    for copy in (dq0, dq1, put_y, put_kv):
-        copy.wait()
 
 
 def per_device(queries, keys_values, grad_layer, out_proj, doc_layout):
@@ -658,7 +650,6 @@
         vm((4, 256, 512), F32),
         vm((4, 256, 512), BF16),
         vm((4, 256, 512), BF16),
-        vm((2, 128, 2048), BF16),
         vm((4, 2, 128, 256), BF16),
         vm((3, 2, 128, 256), F32),
         vm((3, 2, 128, 256), BF16),
@@ -667,26 +658,41 @@
         vm((2, 128, 256), BF16),
         vm((2, 128, 256), BF16),
         vm((2, 128, 256), F32),
-        vm((2, 128, 1024), F32),
-        vm((2, 2, 128, 256), F32),
         dma((8,)), dma((8,)), dma((8,)), dma((72,)), dma((72,)),
         dma((8,)), dma((8,)), dma((4,)), dma((4,)), dma((8,)), dma((8,)),
     ]
     anywhere = pl.BlockSpec(memory_space=pl.ANY)
-    return pl.pallas_call(
+    near = pl.BlockSpec(memory_space=pltpu.VMEM)
+    shapes = (((2, 128, 2048), BF16), ((2, 128, 1024), F32), ((2, 2, 128, 256), F32))
+    results = pl.pallas_call(
         kernel,
-        out_shape=(
-            jax.ShapeDtypeStruct((2, 128, 2048), BF16),
-            jax.ShapeDtypeStruct((2, 128, 1024), F32),
-            jax.ShapeDtypeStruct((2, 2, 128, 256), F32),
-        ),
+        out_shape=tuple(pltpu.VMEM(*shape) for shape in shapes),
         in_specs=[anywhere] * 5,
-        out_specs=(anywhere,) * 3,
+        out_specs=(near,) * 3,
         scratch_shapes=scratch,
         compiler_params=pltpu.CompilerParams(
-            collective_id=0, has_side_effects=True, vmem_limit_bytes=62 * 1024 * 1024
+            collective_id=0, has_side_effects=True, vmem_limit_bytes=56 * 1024 * 1024
         ),
     )(queries, keys_values, grad_layer, out_proj, doc_layout)
+    return pl.pallas_call(
+        put_out,
+        out_shape=tuple(jax.ShapeDtypeStruct(*shape) for shape in shapes),
+        in_specs=[near] * 3,
+        out_specs=(anywhere,) * 3,
+        scratch_shapes=[dma((3,))],
+        compiler_params=pltpu.CompilerParams(vmem_limit_bytes=4 * 1024 * 1024),
+    )(*results)
+
+
+def put_out(a, b, c, out_a, out_b, out_c, sem):
+    copies = [
+        pltpu.make_async_copy(src, target, sem.at[n])
+        for n, (src, target) in enumerate(((a, out_a), (b, out_b), (c, out_c)))
+    ]
+    for copy in copies:
+        copy.start()
+    for copy in copies:
+        copy.wait()
 
 
 def solution(mesh):

time: 75.5 us -> 70.5 us (0.934); the launches traced: 75.3 us -> 69.4 us
  local copies, waits for them, and re-layouts: 4.19 us -> 0 us
  Pallas kernels: 70.5 us -> 68.6 us
    unnamed x7 -> x0, local copies, waits for them, and re-layouts: 4.19 us -> none
    pallas_call x1 -> x2, Pallas kernels: 70.5 us -> 68.6 us  [the longest x1 67 us: per_device(): pl.pallas_call(kernel, out_shape=tuple((pltpu.VMEM(*shape) for shape in s...]
where the time goes in v2:
time: 70.5 us; the launch traced here: 69.4 us
  Pallas kernels  68.6 us (97%)
  between operations  0.8 us (1%)
    pallas_call x1, Pallas kernels, per_device(): pl.pallas_call(kernel, out_shape=tuple((pltpu.VMEM(*shape) for shape in s...  67 us
    pallas_call x1, Pallas kernels, per_device(): pl.pallas_call(put_out, out_shape=tuple((jax.ShapeDtypeStruct(*shape) for...  1.51 us

profile of v2, /device:TPU:7, one launch (start us, length us, event | category | flops | bytes accessed | tf_op | source)
XLA Modules:
  0.0 69.4 jit_solution(819347092718065418)
XLA Ops:
  0.6 67.0 %shard_map.76 = (bf16[2,128,2048]{2,1,0:T(8,128)(2,1)S(1)}, f32[2,128,1024]{2,1,0:T(8,128)S(1)}, f32[2,2,128,256]{3,2,1,0:T(8,128)S(1)}) custom-call(bf16[2,128,1024]{2,1,0:T(8,128)(2,1)} %q_hbm.1, bf16[2,2,128,256]{3,2,1,0:T(8,128)(2,1)} %kv_hbm.1, bf16[2,128,4096]{2,1,0:T(8,128)(2,1)} %g_hbm.1, bf16[32,1024]{1,0:T(8,128)(2,1)} %w_hbm.1, s32[3,128]{1,0:T(4,128)} %lay_hbm.1), custom_call_target="tpu_custom_call" | custom-call | tf_op jit(solution)/shard_map/pallas_call | solution.py:667
  67.7 1.5 %shard_map.77 = (bf16[2,128,2048]{2,1,0:T(8,128)(2,1)}, f32[2,128,1024]{2,1,0:T(8,128)}, f32[2,2,128,256]{3,2,1,0:T(8,128)}) custom-call(bf16[2,128,2048]{2,1,0:T(8,128)(2,1)S(1)} %get-tuple-element.6.a, f32[2,128,1024]{2,1,0:T(8,128)S(1)} %get-tuple-element.7.b, f32[2,2,128,256]{3,2,1,0:T(8,128)S(1)} %get-tuple-element.8.c), custom_call_target="tpu_custom_call" | custom-call | tf_op jit(solution)/shard_map/pallas_call | solution.py:677

commit v3 on v2

--- a/solution.py
+++ b/solution.py
@@ -222,18 +222,18 @@
             [(start_z,), (start, 1, 3)],
             [(mate_first,)],
             [(all_near,)],
-            [(zhop, 0, 1)],
-            [(zhop, 1, 1), (zhop, 2, 1), (give, 0)],
-            [(zhop, 3, 1), (zhop, 0, 2)],
-            [(zhop, 1, 2), (give, 1, 2)],
+            [(zhop, 0, 1), (give, 0)],
+            [(zhop, 1, 1), (zhop, 2, 1)],
+            [(zhop, 3, 1), (give, 1, 2), (zhop, 0, 2)],
+            [(zhop, 1, 2)],
             [(zhop, 2, 2)],
-            [(zhop, 3, 2)],
-            [(zhop, 0, 3), (zhop, 1, 3), (give, 3, 4)],
+            [(zhop, 3, 2), (give, 3, 4)],
+            [(zhop, 0, 3), (zhop, 1, 3)],
             [(zhop, 2, 3)],
-            [(zhop, 3, 3)],
-            [(give, 5, 6), (zhop, 0, 4), (zhop, 1, 4)],
+            [(zhop, 3, 3), (give, 5, 6)],
+            [(zhop, 0, 4), (zhop, 1, 4)],
+            [(zhop, 2, 4), (zhop, 3, 4), (give, 7)],
             [],
-            [(zhop, 2, 4), (zhop, 3, 4), (give, 7)],
             [], [], [],
             [(start, 4, 2, 5, 7, 6)],
         ]
@@ -313,10 +313,10 @@
             [(onward, 1, 5, 6)],
             [(onward, 0, 7), (give, 3, 4)],
             [(onward, 1, 7)],
-            [],
             [(give, 5, 6)],
             [],
             [(give, 7)],
+            [],
             [], [], [], [],
         ]
         return [functools.partial(run, steps) for steps in plan]
@@ -540,6 +540,8 @@
             def _():
                 collect(pair + 2)
 
+    pl.when(core == 1)(functools.partial(collect, 1))
+
     @pl.loop(0, 2)
     def _(group):
         dk, dv = grads(
@@ -562,8 +564,8 @@
                 dqv[copy_id, :, lanes(head)] = result[:, half * 128:(half + 1) * 128].T
 
 
-    pl.when(core == 1)(functools.partial(collect, 1))
     dqueries(0)
+    dqueries(1)
 
     def line_sums():
         for n in (2, 1, 0, 3):
@@ -579,9 +581,6 @@
             back[kind] = other.astype(BF16)
         remote(back, retp, rs.at[7], rr.at[7], dev_before).start()
 
-    line_sums()
-    dqueries(1)
-
     def mine(j):
         for line_id in range(2):
             part = slice(line_id * 256, (line_id + 1) * 256)
@@ -589,6 +588,7 @@
 
     for j in range(4):
         mine(j)
+    line_sums()
 
     def finish(j):
         remote(ysend.at[j], yrecv.at[j], es.at[j], er.at[j], dev_head).wait_recv()

time: 70.5 us -> 70 us (level)
  no operation moved by 1% of the time
where the time goes in v3:
time: 70 us; the launch traced here: 68.8 us
  Pallas kernels  68 us (97%)
  between operations  0.8 us (1%)
    pallas_call x1, Pallas kernels, per_device(): pl.pallas_call(kernel, out_shape=tuple((pltpu.VMEM(*shape) for shape in s...  66.4 us
    pallas_call x1, Pallas kernels, per_device(): pl.pallas_call(put_out, out_shape=tuple((jax.ShapeDtypeStruct(*shape) for...  1.51 us

profile of v3, /device:TPU:7, one launch (start us, length us, event | category | flops | bytes accessed | tf_op | source)
XLA Modules:
  0.0 68.8 jit_solution(4165072650215829993)
XLA Ops:
  0.6 66.4 %shard_map.76 = (bf16[2,128,2048]{2,1,0:T(8,128)(2,1)S(1)}, f32[2,128,1024]{2,1,0:T(8,128)S(1)}, f32[2,2,128,256]{3,2,1,0:T(8,128)S(1)}) custom-call(bf16[2,128,1024]{2,1,0:T(8,128)(2,1)} %q_hbm.1, bf16[2,2,128,256]{3,2,1,0:T(8,128)(2,1)} %kv_hbm.1, bf16[2,128,4096]{2,1,0:T(8,128)(2,1)} %g_hbm.1, bf16[32,1024]{1,0:T(8,128)(2,1)} %w_hbm.1, s32[3,128]{1,0:T(4,128)} %lay_hbm.1), custom_call_target="tpu_custom_call" | custom-call | tf_op jit(solution)/shard_map/pallas_call | solution.py:667
  67.1 1.5 %shard_map.77 = (bf16[2,128,2048]{2,1,0:T(8,128)(2,1)}, f32[2,128,1024]{2,1,0:T(8,128)}, f32[2,2,128,256]{3,2,1,0:T(8,128)}) custom-call(bf16[2,128,2048]{2,1,0:T(8,128)(2,1)S(1)} %get-tuple-element.6.a, f32[2,128,1024]{2,1,0:T(8,128)S(1)} %get-tuple-element.7.b, f32[2,2,128,256]{3,2,1,0:T(8,128)S(1)} %get-tuple-element.8.c), custom_call_target="tpu_custom_call" | custom-call | tf_op jit(solution)/shard_map/pallas_call | solution.py:677
